TPU v7x, 32 devices: a whole 2x2x4 slice. The times are simulated.
32 devices in a mesh: groups: 2 (over x), blk: 16 (over z, y, core).
Axes of the slice: x: 2, y: 2, z: 4, core: 2. Of those that a mesh axis runs over, the one named last changes fastest.
Arguments:
- text_queries: bfloat16 [4096, 4096], P(('groups', 'blk')), parts along dimension 0, may hold values from -170 to 170
- image_states: bfloat16 [1536, 8192], P(('groups', 'blk')), parts along dimension 0, may hold values from -6 to 6
- kv_weight: bfloat16 [8192, 1024], P('blk'), may hold values from -0.1875 to 0.1875
- q_gain: float32 [128], replicated, may hold values from 0.25 to 1.75
- k_gain: float32 [128], replicated, may hold values from 0.25 to 1.75
- text_counts: int32 [6], P('groups'), parts along dimension 0, may hold values from 1 to 1024, 2048 in all
- image_counts: int32 [6], P('groups'), parts along dimension 0, may hold values from 96 to 384, as said below
Outputs:
- attended: bfloat16 [4096, 4096], P(('groups', 'blk')), parts along dimension 0
There are 2 independent parts, one for each index of `groups`. A program takes and returns all parts, laid end to end along the dimension named above; an argument that names none is the same for every part. Nothing has to cross between parts.
Inputs may be any that keep to these rules, and one draw needn't show every extreme that they name: `text_counts`: they sum to 2048. `image_counts`: they sum to 768; the second image has exactly 384 tokens, the first and last are cut by the window.
All inputs are finite; a program needn't handle non-finite values.
Results may differ from a plain program's by a relative error of at most 0.0071.
Values may be sent and summed in bfloat16 or wider, within the bound.
No kernel may reach another device: no remote copies, remote signals or barrier semaphores. Data moves between devices by JAX's collectives and lax.ppermute only.
A program may use at most 128 MiB of HBM per device.

v0:
```python
import math
import jax
import jax.numpy as jnp
from jax import lax
from jax.sharding import PartitionSpec as P

epsilon = 1e-05


def rms_norm(inputs, norm_gain):
    return (
        inputs * lax.rsqrt(jnp.mean(inputs * inputs, axis=-1, keepdims=True) + epsilon) * norm_gain
    )


def body(text_queries, image_states, kv_weight, q_gain, k_gain, text_counts, image_counts):
    head_dim = q_gain.shape[0]
    text_rows = text_queries.shape[0]
    image_rows = image_states.shape[0]
    kv_width = kv_weight.shape[1] // 2
    kv_heads = kv_width // head_dim
    query_heads = text_queries.shape[1] // head_dim
    group_size = query_heads // kv_heads
    columns = lax.all_to_all(image_states, "blk", split_axis=1, concat_axis=0, tiled=True)
    projected = lax.psum_scatter(
        jnp.dot(columns, kv_weight, preferred_element_type=jnp.float32),
        "blk",
        scatter_dimension=0,
        tiled=True,
    )
    image_keys = rms_norm(projected[:, :kv_width].reshape(image_rows, kv_heads, head_dim), k_gain)
    image_keys = image_keys.astype(jnp.bfloat16).reshape(image_rows, kv_width)
    image_values = projected[:, kv_width:].astype(jnp.bfloat16)
    kv_rows_local = jnp.concatenate([image_keys, image_values], axis=1)
    normed_queries = rms_norm(
        text_queries.astype(jnp.float32).reshape(text_rows, query_heads, head_dim), q_gain
    )
    normed_queries = normed_queries.astype(jnp.bfloat16).reshape(
        text_rows, kv_heads, group_size, head_dim
    )
    text_positions = lax.axis_index("blk") * text_rows + jnp.arange(text_rows, dtype=jnp.int32)
    text_ends = jnp.cumsum(text_counts)
    image_ends = jnp.cumsum(image_counts)
    text_segment = jnp.sum(
        (text_ends[None, :] <= text_positions[:, None]).astype(jnp.int32), axis=1
    )
    score_scale = 1.0 / math.sqrt(head_dim)
    arrived = lax.all_gather(kv_rows_local, "blk", axis=0, tiled=True)
    first_row = jnp.int32(0)
    numerator = jnp.zeros((kv_heads, group_size, text_rows, head_dim), jnp.float32)
    denominator = jnp.zeros((kv_heads, group_size, text_rows), jnp.float32)
    key_span = arrived.shape[0]
    for offset in range(0, key_span, 512):
        block_size = min(512, key_span - offset)
        key_block = arrived[offset : offset + block_size]
        key_heads = key_block[:, :kv_width].reshape(block_size, kv_heads, head_dim)
        value_heads = key_block[:, kv_width:].reshape(block_size, kv_heads, head_dim)
        key_positions = first_row + offset + jnp.arange(block_size, dtype=jnp.int32)
        key_owner = jnp.sum(
            (image_ends[None, :] <= key_positions[:, None]).astype(jnp.int32), axis=1
        )
        allowed = key_owner[None, :] <= text_segment[:, None]
        scores = (
            jnp.einsum(
                "tgrd,pgd->grtp", normed_queries, key_heads, preferred_element_type=jnp.float32
            )
            * score_scale
        )
        weights = jnp.where(allowed, jnp.exp(scores), 0.0)
        denominator = denominator + jnp.sum(weights, axis=-1)
        numerator = numerator + jnp.einsum(
            "grtp,pgd->grtd",
            weights.astype(jnp.bfloat16),
            value_heads,
            preferred_element_type=jnp.float32,
        )
    numerator, denominator = (numerator, denominator)
    attended = (numerator / denominator[..., None]).astype(jnp.bfloat16)
    return jnp.transpose(attended, (2, 0, 1, 3)).reshape(text_rows, query_heads * head_dim)


def solution(mesh):
    placed = (
        P(("groups", "blk"), None),
        P(("groups", "blk"), None),
        P("blk", None),
        P(),
        P(),
        P("groups"),
        P("groups"),
    )
    return jax.shard_map(
        body, mesh=mesh, in_specs=placed, out_specs=P(("groups", "blk"), None), check_vma=False
    )
```

profile of v0, /device:TPU:0, one launch (start us, length us, event | category | flops | bytes accessed | tf_op | source)
XLA Modules:
  0.0 173.4 jit_solution(13814516155407754564)
XLA Ops:
  6.5 1.3 copy.124
  7.8 27.3 %all_to_all.19 = bf16[48,16,512]{2,0,1:T(8,128)(2,1)S(1)} all-to-all(bf16[48,16,512]{2,0,1:T(8,128)(2,1)S(1)} %bitcast.70), channel_id=1, replica_groups=mesh['groups'=2,'blk'=16] {'blk'}, dimensions={1} | all-to-all | bytes 1572864 | tf_op jit(solution)/shard_map/all_to_all | solution.py:24
  35.2 2.6 %fusion.34 = f32[768,1024]{1,0:T(8,128)} fusion(bf16[768,512]{1,0:T(8,128)(2,1)S(1)} %bitcast.69, bf16[512,1024]{1,0:T(8,128)(2,1)S(1)} %copy-done), kind=kOutput, calls=%fused_computation.51 | convolution fusion | flops 805306368 | bytes 4980736 | tf_op jit(solution)/shard_map/dot_general | solution.py:26
  37.9 0.6 copy-done.4
  38.5 65.1 %reduce-scatter.2.cloned.1.call-done = f32[48,1024]{1,0:T(8,128)} async-done(((f32[768,1024]{1,0:T(8,128)}), f32[48,1024]{1,0:T(8,128)}) %reduce-scatter.2.cloned.1.call-update) | async-done | bytes 196624 | tf_op jit(solution)/shard_map/reduce_scatter | solution.py:25
  103.6 0.9 slice_multiply_fusion
  104.7 0.9 slice.40
  105.7 0.9 fusion.27
  106.6 0.6 pad_maximum_fusion
  107.9 0.4 copy.101
  108.3 0.6 reduce_sum.66
  108.9 1.4 convert_bitcast_fusion
  111.3 34.7 %all-gather.2.cloned.1.call-done = bf16[768,1024]{1,0:T(8,128)(2,1)} async-done(((bf16[48,1024]{1,0:T(8,128)(2,1)}), bf16[768,1024]{1,0:T(8,128)(2,1)}) %all-gather.2.cloned.1.call-update) | async-done | bytes 1572880 | tf_op jit(solution)/shard_map/all_gather | solution.py:48
  146.0 2.2 %fusion.32 = (bf16[512,512]{1,0:T(8,128)(2,1)}, bf16[512,512]{1,0:T(8,128)(2,1)}) fusion(bf16[768,1024]{1,0:T(8,128)(2,1)} %all-gather.2.cloned.1.call-done), kind=kLoop, calls=%fused_computation.49 | loop fusion | bytes 2097152 | tf_op jit(solution)/shard_map/slice | solution.py:56
  148.3 2.0 %reshape.123 = bf16[512,4,128]{2,1,0:T(4,128)(2,1)} reshape(bf16[512,512]{1,0:T(8,128)(2,1)} %get-tuple-element.5) | data formatting | bytes 1048576 | tf_op jit(solution)/shard_map/reshape | solution.py:56
  150.2 1.8 %fusion.33 = (bf16[256,512]{1,0:T(8,128)(2,1)S(1)}, bf16[256,512]{1,0:T(8,128)(2,1)}) fusion(bf16[768,1024]{1,0:T(8,128)(2,1)} %all-gather.2.cloned.1.call-done), kind=kLoop, calls=%fused_computation.50 | loop fusion | bytes 1048576 | tf_op jit(solution)/shard_map/slice | solution.py:56
  152.0 0.8 reshape.126
  152.8 1.1 copy.97
  153.9 2.0 %copy.94 = bf16[512,512]{0,1:T(8,128)(2,1)} copy(bf16[512,512]{1,0:T(8,128)(2,1)} %get-tuple-element.6) | data formatting | bytes 1048576 | tf_op jit(solution)/shard_map/reshape | solution.py:57
  155.9 3.2 %fusion.7 = (f32[4,8,128]{2,1,0:T(8,128)S(1)}, f32[4,256,128,8]{2,1,3,0:T(8,128)S(1)}) fusion(pred[128,256]{0,1:T(8,128)(4,1)S(1)} %broadcast_compare_fusion.1, f32[128,4,8,128]{3,2,1,0:T(8,128)S(1)} %bitcast.71, f32[128]{0:T(128)S(1)} %copy-done.7, f32[128,4,8]{0,2,1:T(8,128)S(1)} %rsqrt_bitcast_fusion, bf16[256,4,128,1]{2,1,0,3:T(4,128)(2,1)} %bitcast.79), kind=kOutput, calls=%fused_computation.8 | convolution fusion | flops 273149952 | bytes 6619648 | tf_op jit(solution)/shard_map/tgrd,pgd->grtp/dot_general | solution.py:64
  159.1 0.9 fusion.10
  160.2 3.3 %fusion = (f32[4,8,128]{2,1,0:T(8,128)S(1)}, f32[4,512,128,8]{2,1,3,0:T(8,128)S(1)}) fusion(pred[128,512]{0,1:T(8,128)(4,1)S(1)} %broadcast_compare_fusion, f32[128,4,8,128]{3,2,1,0:T(8,128)S(1)} %bitcast.72, f32[128]{0:T(128)S(1)} %copy-done.7, f32[128,4,8]{0,2,1:T(8,128)S(1)} %rsqrt_bitcast_fusion, bf16[512,4,128,1]{2,1,0,3:T(4,128)(2,1)S(1)} %bitcast.76), kind=kOutput, calls=%fused_computation.1 | convolution fusion | flops 544731136 | bytes 11108864 | tf_op jit(solution)/shard_map/tgrd,pgd->grtp/dot_general | solution.py:64
  163.5 1.8 %fusion.12 = bf16[128,4,8,128]{0,3,2,1:T(8,128)(2,1)S(1)} fusion(f32[4,8,128,128]{2,3,1,0:T(8,128)S(1)} %fusion.10, bf16[512,4,128,1]{0,2,3,1:T(8,128)(2,1)S(1)} %bitcast.77, f32[4,512,128,8]{2,1,3,0:T(8,128)S(1)} %get-tuple-element.10, pred[128,512]{0,1:T(8,128)(4,1)S(1)} %broadcast_compare_fusion, f32[128,4,8]{0,2,1:T(8,128)S(1)} %add_bitcast_fusion), kind=kOutput, calls=%fused_computation.15 | convolution fusion | flops 544735232 | bytes 12140544 | tf_op jit(solution)/shard_map/grtp,pgd->grtd/dot_general | solution.py:71
  165.3 1.3 copy.85
  (38 shorter events, 2.1 us)
Async XLA Ops:
  6.5 28.6 %copy-start = (bf16[512,1024]{1,0:T(8,128)(2,1)S(1)}, bf16[512,1024]{1,0:T(8,128)(2,1)}, u32[]{:S(2)}) copy-start(bf16[512,1024]{1,0:T(8,128)(2,1)} %param.9) | copy-start | bytes 3145732
  6.5 97.0 %reduce-scatter.2.cloned.1.call-start = ((), (), s32[]{:S(2)}) async-start(), calls=%async_computation.2 | async-start | bytes 3342336 | tf_op jit(solution)/shard_map/reduce_scatter | solution.py:25
  37.8 0.7 copy-start.4
  37.8 69.5 %copy-start.5 = (s32[3]{0:T(128)S(1)}, s32[3]{0:T(128)}, u32[]{:S(2)}) copy-start(s32[3]{0:T(128)} %param.12) | copy-start | bytes 40
  37.8 69.6 %copy-start.6 = (s32[3]{0:T(128)S(1)}, s32[3]{0:T(128)}, u32[]{:S(2)}) copy-start(s32[3]{0:T(128)} %param.13) | copy-start | bytes 40
  37.8 69.8 %copy-start.1 = (bf16[128,4096]{1,0:T(8,128)(2,1)S(1)}, bf16[128,4096]{1,0:T(8,128)(2,1)}, u32[]{:S(2)}) copy-start(bf16[128,4096]{1,0:T(8,128)(2,1)} %param.7) | copy-start | bytes 3145732
  37.9 108.2 %all-gather.2.cloned.1.call-start = ((), (), s32[]{:S(2)}) async-start(), calls=%async_computation.3 | async-start | bytes 1671168 | tf_op jit(solution)/shard_map/all_gather | solution.py:48
  148.3 7.7 %copy-start.7 = (f32[128]{0:T(128)S(1)}, f32[128]{0:T(128)}, u32[]{:S(2)}) copy-start(f32[128]{0:T(128)} %param.10) | copy-start | bytes 1540
  159.1 1.0 copy-start.2
  160.2 3.3 %copy-start.3 = (bf16[512,512]{0,1:T(8,128)(2,1)S(1)}, bf16[512,512]{0,1:T(8,128)(2,1)}, u32[]{:S(2)}) copy-start(bf16[512,512]{0,1:T(8,128)(2,1)} %copy.94) | copy-start | bytes 1572868
Sparse Core Ops, SparseCore 0:
  38.0 65.5 reduce-scatter.1
  107.4 38.5 all-gather.1
where the time goes:
time: 174 us; the launch traced here: 173 us
  waiting for transfers between devices  99.9 us (57%)
  blocking collectives  27.3 us (16%)
  local copies, waits for them, and re-layouts  15.1 us (9%)
  between operations  13.6 us (8%)
  matrix products  11.8 us (7%)
  other arithmetic  5.74 us (3%)
    reduce_scatter x1, waiting for transfers between devices, body(): lax.psum_scatter(jnp.dot(columns, kv_weight, preferred_element_type=jnp.f...  65.1 us
    all_gather x1, waiting for transfers between devices, body(): arrived = lax.all_gather(kv_rows_local, 'blk', axis=0, tiled=True)  34.7 us
    all_to_all x1, blocking collectives, body(): lax.all_to_all(image_states, 'blk', split_axis=1, concat_axis=0, tiled=True)  27.3 us
    dot_general x2, matrix products, body(): jnp.einsum('tgrd,pgd->grtp', normed_queries, key_heads, preferred_element...  6.52 us
    slice x2, local copies, waits for them, and re-layouts, body(): key_heads = key_block[:, :kv_width].reshape(block_size, kv_heads, head_dim)  4 us
  transfers between devices with their start and end apart: 2, of which 2 were waited for; matrix products, arithmetic and copies ran while one was open for 2% of the time, Pallas kernels for 0%

commit v1 on v0

--- a/solution.py
+++ b/solution.py
@@ -21,7 +21,12 @@
     kv_heads = kv_width // head_dim
     query_heads = text_queries.shape[1] // head_dim
     group_size = query_heads // kv_heads
-    columns = lax.all_to_all(image_states, "blk", split_axis=1, concat_axis=0, tiled=True)
+    columns = jnp.concatenate(
+        lax.all_to_all(
+            jnp.stack(jnp.split(image_states, lax.axis_size("blk"), axis=1)), "blk", 0, 0
+        ),
+        axis=0,
+    )
     projected = lax.psum_scatter(
         jnp.dot(columns, kv_weight, preferred_element_type=jnp.float32),
         "blk",

time: 174 us -> 186 us (1.069)
  local copies, waits for them, and re-layouts: 15.1 us -> 26.7 us
    unnamed x18 -> x33, local copies, waits for them, and re-layouts: 1.5 us -> 13.6 us
where the time goes in v1:
time: 186 us; the launch traced here: 185 us
  waiting for transfers between devices  99.9 us (54%)
  blocking collectives  27.3 us (15%)
  local copies, waits for them, and re-layouts  26.7 us (14%)
  between operations  13.6 us (7%)
  matrix products  11.8 us (6%)
  other arithmetic  5.74 us (3%)
    reduce_scatter x1, waiting for transfers between devices, body(): lax.psum_scatter(jnp.dot(columns, kv_weight, preferred_element_type=jnp.f...  65.3 us
    all_gather x1, waiting for transfers between devices, body(): arrived = lax.all_gather(kv_rows_local, 'blk', axis=0, tiled=True)  34.6 us
    all_to_all x1, blocking collectives, body(): lax.all_to_all(jnp.stack(jnp.split(image_states, lax.axis_size('blk'), ax...  27.3 us
    unnamed x33, local copies, waits for them, and re-layouts  13.6 us
    dot_general x2, matrix products, body(): jnp.einsum('tgrd,pgd->grtp', normed_queries, key_heads, preferred_element...  6.51 us
    slice x2, local copies, waits for them, and re-layouts, body(): key_heads = key_block[:, :kv_width].reshape(block_size, kv_heads, head_dim)  4 us
  transfers between devices with their start and end apart: 2, of which 2 were waited for; matrix products, arithmetic and copies ran while one was open for 2% of the time, Pallas kernels for 0%

profile of v1, /device:TPU:0, one launch (start us, length us, event | category | flops | bytes accessed | tf_op | source)
XLA Modules:
  0.0 185.0 jit_solution(4490768292273107785)
XLA Ops:
  6.5 0.9 bitcast_dynamic-update-slice_fusion.15
  7.4 0.8 bitcast_dynamic-update-slice_fusion.14
  8.2 0.8 bitcast_dynamic-update-slice_fusion.13
  9.0 0.8 bitcast_dynamic-update-slice_fusion.12
  9.8 0.8 bitcast_dynamic-update-slice_fusion.11
  11.4 0.8 bitcast_dynamic-update-slice_fusion.9
  19.5 27.3 %all_to_all.5 = bf16[16,48,512]{2,1,0:T(8,128)(2,1)S(1)} all-to-all(bf16[16,48,512]{2,1,0:T(8,128)(2,1)S(1)} %bitcast_dynamic-update-slice_fusion), channel_id=1, replica_groups=mesh['groups'=2,'blk'=16] {'blk'}, dimensions={0} | all-to-all | bytes 1572864 | tf_op jit(solution)/shard_map/all_to_all | solution.py:25
  46.8 2.6 %fusion.34 = f32[768,1024]{1,0:T(8,128)} fusion(bf16[768,512]{1,0:T(8,128)(2,1)S(1)} %bitcast.95, bf16[512,1024]{1,0:T(8,128)(2,1)S(1)} %copy-done), kind=kOutput, calls=%fused_computation.66 | convolution fusion | flops 805306368 | bytes 4980736 | tf_op jit(solution)/shard_map/dot_general | solution.py:31
  50.1 65.3 %reduce-scatter.2.cloned.1.call-done = f32[48,1024]{1,0:T(8,128)} async-done(((f32[768,1024]{1,0:T(8,128)}), f32[48,1024]{1,0:T(8,128)}) %reduce-scatter.2.cloned.1.call-update) | async-done | bytes 196624 | tf_op jit(solution)/shard_map/reduce_scatter | solution.py:30
  115.4 0.9 slice_multiply_fusion
  116.5 0.9 slice.40
  117.5 0.9 fusion.27
  120.7 1.4 convert_bitcast_fusion
  123.1 34.6 %all-gather.2.cloned.1.call-done = bf16[768,1024]{1,0:T(8,128)(2,1)} async-done(((bf16[48,1024]{1,0:T(8,128)(2,1)}), bf16[768,1024]{1,0:T(8,128)(2,1)}) %all-gather.2.cloned.1.call-update) | async-done | bytes 1572880 | tf_op jit(solution)/shard_map/all_gather | solution.py:53
  157.7 2.2 %fusion.32 = (bf16[512,512]{1,0:T(8,128)(2,1)}, bf16[512,512]{1,0:T(8,128)(2,1)}) fusion(bf16[768,1024]{1,0:T(8,128)(2,1)} %all-gather.2.cloned.1.call-done), kind=kLoop, calls=%fused_computation.64 | loop fusion | bytes 2097152 | tf_op jit(solution)/shard_map/slice | solution.py:61
  159.9 2.0 %reshape.124 = bf16[512,4,128]{2,1,0:T(4,128)(2,1)} reshape(bf16[512,512]{1,0:T(8,128)(2,1)} %get-tuple-element.5) | data formatting | bytes 1048576 | tf_op jit(solution)/shard_map/reshape | solution.py:61
  161.9 1.8 fusion.33
  164.4 1.1 copy.75
  165.5 2.0 %copy.72 = bf16[512,512]{0,1:T(8,128)(2,1)} copy(bf16[512,512]{1,0:T(8,128)(2,1)} %get-tuple-element.6) | data formatting | bytes 1048576 | tf_op jit(solution)/shard_map/reshape | solution.py:62
  167.5 3.2 %fusion.7 = (f32[4,8,128]{2,1,0:T(8,128)S(1)}, f32[4,256,128,8]{2,1,3,0:T(8,128)S(1)}) fusion(pred[128,256]{0,1:T(8,128)(4,1)S(1)} %broadcast_compare_fusion.1, f32[128,4,8,128]{3,2,1,0:T(8,128)S(1)} %bitcast.96, f32[128]{0:T(128)S(1)} %copy-done.7, f32[128,4,8]{0,2,1:T(8,128)S(1)} %rsqrt_bitcast_fusion, bf16[256,4,128,1]{2,1,0,3:T(4,128)(2,1)} %bitcast.103), kind=kOutput, calls=%fused_computation.8 | convolution fusion | flops 273149952 | bytes 6619648 | tf_op jit(solution)/shard_map/tgrd,pgd->grtp/dot_general | solution.py:69
  170.8 0.9 fusion.10
  171.8 3.3 %fusion = (f32[4,8,128]{2,1,0:T(8,128)S(1)}, f32[4,512,128,8]{2,1,3,0:T(8,128)S(1)}) fusion(pred[128,512]{0,1:T(8,128)(4,1)S(1)} %broadcast_compare_fusion, f32[128,4,8,128]{3,2,1,0:T(8,128)S(1)} %bitcast.97, f32[128]{0:T(128)S(1)} %copy-done.7, f32[128,4,8]{0,2,1:T(8,128)S(1)} %rsqrt_bitcast_fusion, bf16[512,4,128,1]{2,1,0,3:T(4,128)(2,1)S(1)} %bitcast.100), kind=kOutput, calls=%fused_computation.1 | convolution fusion | flops 544731136 | bytes 11108864 | tf_op jit(solution)/shard_map/tgrd,pgd->grtp/dot_general | solution.py:69
  175.1 1.8 fusion.12
  176.9 1.3 copy.63
  (53 shorter events, 13.0 us)
Async XLA Ops:
  6.5 40.3 %copy-start = (bf16[512,1024]{1,0:T(8,128)(2,1)S(1)}, bf16[512,1024]{1,0:T(8,128)(2,1)}, u32[]{:S(2)}) copy-start(bf16[512,1024]{1,0:T(8,128)(2,1)} %param.9) | copy-start | bytes 3145732
  6.5 108.8 %reduce-scatter.2.cloned.1.call-start = ((), (), s32[]{:S(2)}) async-start(), calls=%async_computation.2 | async-start | bytes 3342336 | tf_op jit(solution)/shard_map/reduce_scatter | solution.py:30
  49.4 0.7 copy-start.4
  49.4 69.6 %copy-start.5 = (s32[3]{0:T(128)S(1)}, s32[3]{0:T(128)}, u32[]{:S(2)}) copy-start(s32[3]{0:T(128)} %param.12) | copy-start | bytes 40
  49.4 69.8 %copy-start.6 = (s32[3]{0:T(128)S(1)}, s32[3]{0:T(128)}, u32[]{:S(2)}) copy-start(s32[3]{0:T(128)} %param.13) | copy-start | bytes 40
  49.4 70.0 %copy-start.1 = (bf16[128,4096]{1,0:T(8,128)(2,1)S(1)}, bf16[128,4096]{1,0:T(8,128)(2,1)}, u32[]{:S(2)}) copy-start(bf16[128,4096]{1,0:T(8,128)(2,1)} %param.7) | copy-start | bytes 3145732
  49.5 108.2 %all-gather.2.cloned.1.call-start = ((), (), s32[]{:S(2)}) async-start(), calls=%async_computation.3 | async-start | bytes 1671168 | tf_op jit(solution)/shard_map/all_gather | solution.py:53
  159.9 7.7 %copy-start.7 = (f32[128]{0:T(128)S(1)}, f32[128]{0:T(128)}, u32[]{:S(2)}) copy-start(f32[128]{0:T(128)} %param.10) | copy-start | bytes 1540
  170.8 1.0 copy-start.2
  171.8 3.3 %copy-start.3 = (bf16[512,512]{0,1:T(8,128)(2,1)S(1)}, bf16[512,512]{0,1:T(8,128)(2,1)}, u32[]{:S(2)}) copy-start(bf16[512,512]{0,1:T(8,128)(2,1)} %copy.72) | copy-start | bytes 1572868
Sparse Core Ops, SparseCore 0:
  49.6 65.7 reduce-scatter.1
  119.2 38.4 all-gather.1
